TPU v7x, 32 devices: a whole 2x2x4 slice. The times are simulated.
32 devices in a mesh: tm: 8 (over z, y), rep: 4 (over x, core).
Axes of the slice: x: 2, y: 2, z: 4, core: 2. Of those that a mesh axis runs over, the one named last changes fastest.
Arguments:
- transitions: float32 [32, 512, 512], P(('rep', 'tm')), parts along dimension 0, may hold values from -1 to 1, as said below
- cond_covs: float32 [32, 512, 512], P(('rep', 'tm')), parts along dimension 0, may hold values from -40 to 40, as said below
- transition_est: float32 [2048, 512], P('rep'), parts along dimension 0, may hold values from -0.25 to 0.25
Outputs:
- cov_blocks: float32 [32, 512, 512], P(('rep', 'tm')), parts along dimension 0
- transition_grad: float32 [2048, 512], P('rep'), parts along dimension 0
There are 4 independent parts, one for each index of `rep`. A program takes and returns all parts, laid end to end along the dimension named above; each array names one. Nothing has to cross between parts.
Inputs may be any that keep to these rules, and one draw needn't show every extreme that they name: `transitions`: every block has spectral norm below one. `cond_covs`: every block is symmetric and positive definite.
All inputs are finite; a program needn't handle non-finite values.
Results may differ from a plain program's by a relative error of at most 0.00017.
Values sent between devices are 32-bit elements; how exact they have to be, the bound alone decides.
A program may use at most 192 MiB of HBM per device.

v0:
```python
import jax
import jax.numpy as jnp
from jax import lax
from jax.sharding import PartitionSpec as P

highest = lax.Precision.HIGHEST


def passed_along(block, axis, distance):
    devices = range(lax.axis_size(axis))
    route = [(i - distance, i) for i in devices if i - distance in devices]
    return lax.ppermute(block, axis, route)


def times_transposed(left, right):
    return lax.dot_general(
        left, right, (((1,), (1,)), ((), ())), precision=highest, preferred_element_type=jnp.float32
    )


def product(left, right):
    return jnp.dot(left, right, precision=highest, preferred_element_type=jnp.float32)


def on_device(transitions, cond_covs, transition_est):
    blocks_here = transitions.shape[0]
    width = transitions.shape[1]
    devices = lax.axis_size("tm")
    total_blocks = blocks_here * devices
    position = lax.axis_index("tm")
    combined_gain = transitions[blocks_here - 1]
    combined_noise = cond_covs[blocks_here - 1]
    empty_block = jnp.zeros((width, width), jnp.float32)

    def advance(turn_number, incoming):
        outgoing = (
            product(combined_gain, times_transposed(incoming, combined_gain)) + combined_noise
        )
        return passed_along(outgoing, "tm", -1)

    covariance = lax.fori_loop(0, devices - 1, advance, empty_block)
    transition = transitions[0]
    previous_step_cross = times_transposed(covariance, transition)
    covariance = product(transition, previous_step_cross) + cond_covs[0]
    collected = [covariance]
    current_entry = jnp.where(position * blocks_here + 0 < total_blocks - 1, 1.0, 0.0).astype(
        jnp.float32
    )
    accumulated = current_entry * (previous_step_cross - product(transition_est, covariance))
    gradient = lax.psum(accumulated, "tm") / (total_blocks - 1)
    cov_blocks = jnp.stack(collected[::-1], axis=0)
    return (cov_blocks, gradient)


def solution(mesh):
    return jax.shard_map(
        on_device,
        mesh=mesh,
        in_specs=(P(("rep", "tm"), None, None), P(("rep", "tm"), None, None), P("rep", None)),
        out_specs=(P(("rep", "tm"), None, None), P("rep", None)),
        check_vma=False,
    )
```

profile of v0, /device:TPU:26, one launch (start us, length us, event | category | flops | bytes accessed | tf_op | source)
XLA Modules:
  0.0 342.2 jit_solution(12036947720468812156)
XLA Ops:
  7.2 0.0 copy-start
  7.2 0.0 all-reduce.2.cloned.1.call-start
  7.2 2.6 copy.5
  9.8 0.1 broadcast_in_dim.3
  10.0 1.1 copy-done.1
  11.1 231.0 %while.10 = (s32[]{:T(128)}, f32[512,512]{0,1:T(8,128)S(1)}, f32[512,512]{1,0:T(8,128)S(1)}, f32[512,512]{0,1:T(8,128)}, s32[]{:T(128)}) while((s32[]{:T(128)}, f32[512,512]{0,1:T(8,128)S(1)}, f32[512,512]{1,0:T(8,128)S(1)}, f32[512,512]{0,1:T(8,128)}, s32[]{:T(128)}) %tuple.29), condition=%wide.region_1.0_spmd, body=%wide.region_0.0_spmd.sunk | while | flops 3221487616 | bytes 15728769 | solution.py:41
  11.1 3.5 %fusion.26 = f32[512,512]{1,0:T(8,128)S(1)} fusion(f32[512,512]{0,1:T(8,128)S(1)} %get-tuple-element.66, f32[512,512]{1,0:T(8,128)S(1)} %get-tuple-element.72), kind=kOutput, calls=%fused_computation.11.clone.1 | convolution fusion | flops 1610612736 | bytes 3145728 | tf_op jit(solution)/shard_map/while/body/eval_jaxpr/dot_general | solution.py:16
  14.5 0.0 copy-done.2
  14.6 4.4 %fusion.27 = f32[512,512]{0,1:T(8,128)} fusion(f32[512,512]{0,1:T(8,128)S(1)} %copy-done.2, f32[512,512]{1,0:T(8,128)S(1)} %fusion.26, f32[512,512]{1,0:T(8,128)S(1)} %get-tuple-element.72), kind=kOutput, calls=%fused_computation.1.clone.1 | convolution fusion | flops 1610874880 | bytes 4194304 | tf_op jit(solution)/shard_map/while/body/eval_jaxpr/dot_general | solution.py:22
  19.0 3.3 collective-permute-start
  22.3 23.7 %collective-permute-done = f32[512,512]{0,1:T(8,128)S(1)} collective-permute-done((f32[512,512]{0,1:T(8,128)}, f32[512,512]{0,1:T(8,128)S(1)}, u32[]{:S(2)}, u32[]{:S(2)}) %collective-permute-start) | collective-permute-done | bytes 1048608 | tf_op jit(solution)/shard_map/while/body/eval_jaxpr/ppermute | solution.py:12
  46.0 3.5 %fusion.26 = f32[512,512]{1,0:T(8,128)S(1)} fusion(f32[512,512]{0,1:T(8,128)S(1)} %get-tuple-element.66, f32[512,512]{1,0:T(8,128)S(1)} %get-tuple-element.72), kind=kOutput, calls=%fused_computation.11.clone.1 | convolution fusion | flops 1610612736 | bytes 3145728 | tf_op jit(solution)/shard_map/while/body/eval_jaxpr/dot_general | solution.py:16
  49.5 0.0 copy-done.2
  49.5 4.4 %fusion.27 = f32[512,512]{0,1:T(8,128)} fusion(f32[512,512]{0,1:T(8,128)S(1)} %copy-done.2, f32[512,512]{1,0:T(8,128)S(1)} %fusion.26, f32[512,512]{1,0:T(8,128)S(1)} %get-tuple-element.72), kind=kOutput, calls=%fused_computation.1.clone.1 | convolution fusion | flops 1610874880 | bytes 4194304 | tf_op jit(solution)/shard_map/while/body/eval_jaxpr/dot_general | solution.py:22
  53.9 4.2 %collective-permute-start = (f32[512,512]{0,1:T(8,128)}, f32[512,512]{0,1:T(8,128)S(1)}, u32[]{:S(2)}, u32[]{:S(2)}) collective-permute-start(f32[512,512]{0,1:T(8,128)} %fusion.27), channel_id=1, source_target_pairs={{4,0},{8,4},{12,8},{16,12},{20,16},{24,20},{28,24},{5,1},{9,5},{13... | collective-permute-start | bytes 3145736 | tf_op jit(solution)/shard_map/while/body/eval_jaxpr/ppermute | solution.py:12
  58.1 21.9 %collective-permute-done = f32[512,512]{0,1:T(8,128)S(1)} collective-permute-done((f32[512,512]{0,1:T(8,128)}, f32[512,512]{0,1:T(8,128)S(1)}, u32[]{:S(2)}, u32[]{:S(2)}) %collective-permute-start) | collective-permute-done | bytes 1048608 | tf_op jit(solution)/shard_map/while/body/eval_jaxpr/ppermute | solution.py:12
  80.1 3.5 %fusion.26 = f32[512,512]{1,0:T(8,128)S(1)} fusion(f32[512,512]{0,1:T(8,128)S(1)} %get-tuple-element.66, f32[512,512]{1,0:T(8,128)S(1)} %get-tuple-element.72), kind=kOutput, calls=%fused_computation.11.clone.1 | convolution fusion | flops 1610612736 | bytes 3145728 | tf_op jit(solution)/shard_map/while/body/eval_jaxpr/dot_general | solution.py:16
  83.5 0.0 copy-done.2
  83.6 4.4 %fusion.27 = f32[512,512]{0,1:T(8,128)} fusion(f32[512,512]{0,1:T(8,128)S(1)} %copy-done.2, f32[512,512]{1,0:T(8,128)S(1)} %fusion.26, f32[512,512]{1,0:T(8,128)S(1)} %get-tuple-element.72), kind=kOutput, calls=%fused_computation.1.clone.1 | convolution fusion | flops 1610874880 | bytes 4194304 | tf_op jit(solution)/shard_map/while/body/eval_jaxpr/dot_general | solution.py:22
  88.0 5.1 %collective-permute-start = (f32[512,512]{0,1:T(8,128)}, f32[512,512]{0,1:T(8,128)S(1)}, u32[]{:S(2)}, u32[]{:S(2)}) collective-permute-start(f32[512,512]{0,1:T(8,128)} %fusion.27), channel_id=1, source_target_pairs={{4,0},{8,4},{12,8},{16,12},{20,16},{24,20},{28,24},{5,1},{9,5},{13... | collective-permute-start | bytes 3145736 | tf_op jit(solution)/shard_map/while/body/eval_jaxpr/ppermute | solution.py:12
  93.1 21.0 %collective-permute-done = f32[512,512]{0,1:T(8,128)S(1)} collective-permute-done((f32[512,512]{0,1:T(8,128)}, f32[512,512]{0,1:T(8,128)S(1)}, u32[]{:S(2)}, u32[]{:S(2)}) %collective-permute-start) | collective-permute-done | bytes 1048608 | tf_op jit(solution)/shard_map/while/body/eval_jaxpr/ppermute | solution.py:12
  114.1 3.5 %fusion.26 = f32[512,512]{1,0:T(8,128)S(1)} fusion(f32[512,512]{0,1:T(8,128)S(1)} %get-tuple-element.66, f32[512,512]{1,0:T(8,128)S(1)} %get-tuple-element.72), kind=kOutput, calls=%fused_computation.11.clone.1 | convolution fusion | flops 1610612736 | bytes 3145728 | tf_op jit(solution)/shard_map/while/body/eval_jaxpr/dot_general | solution.py:16
  117.6 0.0 copy-done.2
  117.6 4.4 %fusion.27 = f32[512,512]{0,1:T(8,128)} fusion(f32[512,512]{0,1:T(8,128)S(1)} %copy-done.2, f32[512,512]{1,0:T(8,128)S(1)} %fusion.26, f32[512,512]{1,0:T(8,128)S(1)} %get-tuple-element.72), kind=kOutput, calls=%fused_computation.1.clone.1 | convolution fusion | flops 1610874880 | bytes 4194304 | tf_op jit(solution)/shard_map/while/body/eval_jaxpr/dot_general | solution.py:22
  122.1 5.2 %collective-permute-start = (f32[512,512]{0,1:T(8,128)}, f32[512,512]{0,1:T(8,128)S(1)}, u32[]{:S(2)}, u32[]{:S(2)}) collective-permute-start(f32[512,512]{0,1:T(8,128)} %fusion.27), channel_id=1, source_target_pairs={{4,0},{8,4},{12,8},{16,12},{20,16},{24,20},{28,24},{5,1},{9,5},{13... | collective-permute-start | bytes 3145736 | tf_op jit(solution)/shard_map/while/body/eval_jaxpr/ppermute | solution.py:12
  127.2 20.1 %collective-permute-done = f32[512,512]{0,1:T(8,128)S(1)} collective-permute-done((f32[512,512]{0,1:T(8,128)}, f32[512,512]{0,1:T(8,128)S(1)}, u32[]{:S(2)}, u32[]{:S(2)}) %collective-permute-start) | collective-permute-done | bytes 1048608 | tf_op jit(solution)/shard_map/while/body/eval_jaxpr/ppermute | solution.py:12
  147.4 3.5 %fusion.26 = f32[512,512]{1,0:T(8,128)S(1)} fusion(f32[512,512]{0,1:T(8,128)S(1)} %get-tuple-element.66, f32[512,512]{1,0:T(8,128)S(1)} %get-tuple-element.72), kind=kOutput, calls=%fused_computation.11.clone.1 | convolution fusion | flops 1610612736 | bytes 3145728 | tf_op jit(solution)/shard_map/while/body/eval_jaxpr/dot_general | solution.py:16
  150.9 4.4 %fusion.27 = f32[512,512]{0,1:T(8,128)} fusion(f32[512,512]{0,1:T(8,128)S(1)} %copy-done.2, f32[512,512]{1,0:T(8,128)S(1)} %fusion.26, f32[512,512]{1,0:T(8,128)S(1)} %get-tuple-element.72), kind=kOutput, calls=%fused_computation.1.clone.1 | convolution fusion | flops 1610874880 | bytes 4194304 | tf_op jit(solution)/shard_map/while/body/eval_jaxpr/dot_general | solution.py:22
  155.3 5.2 %collective-permute-start = (f32[512,512]{0,1:T(8,128)}, f32[512,512]{0,1:T(8,128)S(1)}, u32[]{:S(2)}, u32[]{:S(2)}) collective-permute-start(f32[512,512]{0,1:T(8,128)} %fusion.27), channel_id=1, source_target_pairs={{4,0},{8,4},{12,8},{16,12},{20,16},{24,20},{28,24},{5,1},{9,5},{13... | collective-permute-start | bytes 3145736 | tf_op jit(solution)/shard_map/while/body/eval_jaxpr/ppermute | solution.py:12
  160.5 19.3 %collective-permute-done = f32[512,512]{0,1:T(8,128)S(1)} collective-permute-done((f32[512,512]{0,1:T(8,128)}, f32[512,512]{0,1:T(8,128)S(1)}, u32[]{:S(2)}, u32[]{:S(2)}) %collective-permute-start) | collective-permute-done | bytes 1048608 | tf_op jit(solution)/shard_map/while/body/eval_jaxpr/ppermute | solution.py:12
  179.8 3.5 %fusion.26 = f32[512,512]{1,0:T(8,128)S(1)} fusion(f32[512,512]{0,1:T(8,128)S(1)} %get-tuple-element.66, f32[512,512]{1,0:T(8,128)S(1)} %get-tuple-element.72), kind=kOutput, calls=%fused_computation.11.clone.1 | convolution fusion | flops 1610612736 | bytes 3145728 | tf_op jit(solution)/shard_map/while/body/eval_jaxpr/dot_general | solution.py:16
  183.3 4.4 %fusion.27 = f32[512,512]{0,1:T(8,128)} fusion(f32[512,512]{0,1:T(8,128)S(1)} %copy-done.2, f32[512,512]{1,0:T(8,128)S(1)} %fusion.26, f32[512,512]{1,0:T(8,128)S(1)} %get-tuple-element.72), kind=kOutput, calls=%fused_computation.1.clone.1 | convolution fusion | flops 1610874880 | bytes 4194304 | tf_op jit(solution)/shard_map/while/body/eval_jaxpr/dot_general | solution.py:22
  187.7 5.2 %collective-permute-start = (f32[512,512]{0,1:T(8,128)}, f32[512,512]{0,1:T(8,128)S(1)}, u32[]{:S(2)}, u32[]{:S(2)}) collective-permute-start(f32[512,512]{0,1:T(8,128)} %fusion.27), channel_id=1, source_target_pairs={{4,0},{8,4},{12,8},{16,12},{20,16},{24,20},{28,24},{5,1},{9,5},{13... | collective-permute-start | bytes 3145736 | tf_op jit(solution)/shard_map/while/body/eval_jaxpr/ppermute | solution.py:12
  192.9 18.4 %collective-permute-done = f32[512,512]{0,1:T(8,128)S(1)} collective-permute-done((f32[512,512]{0,1:T(8,128)}, f32[512,512]{0,1:T(8,128)S(1)}, u32[]{:S(2)}, u32[]{:S(2)}) %collective-permute-start) | collective-permute-done | bytes 1048608 | tf_op jit(solution)/shard_map/while/body/eval_jaxpr/ppermute | solution.py:12
  211.3 3.5 %fusion.26 = f32[512,512]{1,0:T(8,128)S(1)} fusion(f32[512,512]{0,1:T(8,128)S(1)} %get-tuple-element.66, f32[512,512]{1,0:T(8,128)S(1)} %get-tuple-element.72), kind=kOutput, calls=%fused_computation.11.clone.1 | convolution fusion | flops 1610612736 | bytes 3145728 | tf_op jit(solution)/shard_map/while/body/eval_jaxpr/dot_general | solution.py:16
  214.8 4.4 %fusion.27 = f32[512,512]{0,1:T(8,128)} fusion(f32[512,512]{0,1:T(8,128)S(1)} %copy-done.2, f32[512,512]{1,0:T(8,128)S(1)} %fusion.26, f32[512,512]{1,0:T(8,128)S(1)} %get-tuple-element.72), kind=kOutput, calls=%fused_computation.1.clone.1 | convolution fusion | flops 1610874880 | bytes 4194304 | tf_op jit(solution)/shard_map/while/body/eval_jaxpr/dot_general | solution.py:22
  219.3 5.2 %collective-permute-start = (f32[512,512]{0,1:T(8,128)}, f32[512,512]{0,1:T(8,128)S(1)}, u32[]{:S(2)}, u32[]{:S(2)}) collective-permute-start(f32[512,512]{0,1:T(8,128)} %fusion.27), channel_id=1, source_target_pairs={{4,0},{8,4},{12,8},{16,12},{20,16},{24,20},{28,24},{5,1},{9,5},{13... | collective-permute-start | bytes 3145736 | tf_op jit(solution)/shard_map/while/body/eval_jaxpr/ppermute | solution.py:12
  224.5 17.6 %collective-permute-done = f32[512,512]{0,1:T(8,128)S(1)} collective-permute-done((f32[512,512]{0,1:T(8,128)}, f32[512,512]{0,1:T(8,128)S(1)}, u32[]{:S(2)}, u32[]{:S(2)}) %collective-permute-start) | collective-permute-done | bytes 1048608 | tf_op jit(solution)/shard_map/while/body/eval_jaxpr/ppermute | solution.py:12
  242.0 3.5 %fusion.5 = f32[512,512]{1,0:T(8,128)S(1)} fusion(f32[512,512]{0,1:T(8,128)S(1)} %get-tuple-element.24, f32[1,512,512]{2,1,0:T(8,128)S(1)} %bitcast.41), kind=kOutput, calls=%fused_computation.9 | convolution fusion | flops 1610612736 | bytes 3145728 | tf_op jit(solution)/shard_map/dot_general | solution.py:16
  245.5 0.0 copy-start.4
  245.5 1.0 copy-done.4
  246.5 0.0 copy-done.3
  246.5 3.5 %fusion.3 = f32[512,512]{0,1:T(8,128)S(1)} fusion(f32[512,512]{1,0:T(8,128)S(1)} %fusion.5, f32[1,512,512]{1,2,0:T(8,128)S(1)} %bitcast.44, f32[1,512,512]{2,1,0:T(8,128)S(1)} %bitcast.42), kind=kOutput, calls=%fused_computation.6 | convolution fusion | flops 1610874880 | bytes 4194304 | tf_op jit(solution)/shard_map/dot_general | solution.py:22
  250.0 4.1 %fusion.2 = f32[512,512]{1,0:T(8,128)} fusion(f32[512,512]{1,0:T(8,128)} %copy-done.4, f32[512,512]{0,1:T(8,128)S(1)} %fusion.3, f32[512,512]{1,0:T(8,128)S(1)} %copy-done, f32[]{:T(128)S(6)} %select_n.4), kind=kOutput, calls=%fused_computation.4 | convolution fusion | flops 1611137024 | bytes 4194308 | tf_op jit(solution)/shard_map/dot_general | solution.py:22
  254.0 0.0 all-reduce.2.cloned.1.call-update
  254.1 1.3 copy.7
  255.4 77.7 %all-reduce.2.cloned.1.call-done = f32[512,512]{1,0:T(8,128)} async-done(((f32[512,512]{1,0:T(8,128)}), f32[512,512]{1,0:T(8,128)}) %all-reduce.2.cloned.1.call-update) | async-done | bytes 1048592 | tf_op jit(solution)/shard_map/psum | solution.py:50
  333.1 2.3 broadcast_multiply_fusion
  (13 shorter events, 0.0 us)
Async XLA Ops:
  7.2 242.8 %copy-start = (f32[512,512]{1,0:T(8,128)S(1)}, f32[512,512]{1,0:T(8,128)}, u32[]{:S(2)}) copy-start(f32[512,512]{1,0:T(8,128)} %param.7) | copy-start | bytes 3145732
  7.2 325.9 %all-reduce.2.cloned.1.call-start = ((), (), s32[]{:S(2)}) async-start(), calls=%async_computation | async-start | bytes 2097152 | tf_op jit(solution)/shard_map/psum | solution.py:50
  9.8 1.2 copy-start.1
  11.1 3.5 %copy-start.2 = (f32[512,512]{0,1:T(8,128)S(1)}, f32[512,512]{0,1:T(8,128)}, u32[]{:S(2)}) copy-start(f32[512,512]{0,1:T(8,128)} %get-tuple-element.73) | copy-start | bytes 3145732 | tf_op jit(solution)/shard_map/while
  19.0 27.0 %collective-permute-start = (f32[512,512]{0,1:T(8,128)}, f32[512,512]{0,1:T(8,128)S(1)}, u32[]{:S(2)}, u32[]{:S(2)}) collective-permute-start(f32[512,512]{0,1:T(8,128)} %fusion.27), channel_id=1, source_target_pairs={{4,0},{8,4},{12,8},{16,12},{20,16},{24,20},{28,24},{5,1},{9,5},{13... | collective-permute-start | bytes 3145736 | tf_op jit(solution)/shard_map/while/body/eval_jaxpr/ppermute | solution.py:12
  46.0 3.5 %copy-start.2 = (f32[512,512]{0,1:T(8,128)S(1)}, f32[512,512]{0,1:T(8,128)}, u32[]{:S(2)}) copy-start(f32[512,512]{0,1:T(8,128)} %get-tuple-element.73) | copy-start | bytes 3145732 | tf_op jit(solution)/shard_map/while
  53.9 26.1 %collective-permute-start = (f32[512,512]{0,1:T(8,128)}, f32[512,512]{0,1:T(8,128)S(1)}, u32[]{:S(2)}, u32[]{:S(2)}) collective-permute-start(f32[512,512]{0,1:T(8,128)} %fusion.27), channel_id=1, source_target_pairs={{4,0},{8,4},{12,8},{16,12},{20,16},{24,20},{28,24},{5,1},{9,5},{13... | collective-permute-start | bytes 3145736 | tf_op jit(solution)/shard_map/while/body/eval_jaxpr/ppermute | solution.py:12
  80.1 3.5 %copy-start.2 = (f32[512,512]{0,1:T(8,128)S(1)}, f32[512,512]{0,1:T(8,128)}, u32[]{:S(2)}) copy-start(f32[512,512]{0,1:T(8,128)} %get-tuple-element.73) | copy-start | bytes 3145732 | tf_op jit(solution)/shard_map/while
  88.0 26.1 %collective-permute-start = (f32[512,512]{0,1:T(8,128)}, f32[512,512]{0,1:T(8,128)S(1)}, u32[]{:S(2)}, u32[]{:S(2)}) collective-permute-start(f32[512,512]{0,1:T(8,128)} %fusion.27), channel_id=1, source_target_pairs={{4,0},{8,4},{12,8},{16,12},{20,16},{24,20},{28,24},{5,1},{9,5},{13... | collective-permute-start | bytes 3145736 | tf_op jit(solution)/shard_map/while/body/eval_jaxpr/ppermute | solution.py:12
  114.1 3.5 %copy-start.2 = (f32[512,512]{0,1:T(8,128)S(1)}, f32[512,512]{0,1:T(8,128)}, u32[]{:S(2)}) copy-start(f32[512,512]{0,1:T(8,128)} %get-tuple-element.73) | copy-start | bytes 3145732 | tf_op jit(solution)/shard_map/while
  122.1 25.3 %collective-permute-start = (f32[512,512]{0,1:T(8,128)}, f32[512,512]{0,1:T(8,128)S(1)}, u32[]{:S(2)}, u32[]{:S(2)}) collective-permute-start(f32[512,512]{0,1:T(8,128)} %fusion.27), channel_id=1, source_target_pairs={{4,0},{8,4},{12,8},{16,12},{20,16},{24,20},{28,24},{5,1},{9,5},{13... | collective-permute-start | bytes 3145736 | tf_op jit(solution)/shard_map/while/body/eval_jaxpr/ppermute | solution.py:12
  147.4 3.5 %copy-start.2 = (f32[512,512]{0,1:T(8,128)S(1)}, f32[512,512]{0,1:T(8,128)}, u32[]{:S(2)}) copy-start(f32[512,512]{0,1:T(8,128)} %get-tuple-element.73) | copy-start | bytes 3145732 | tf_op jit(solution)/shard_map/while
  155.3 24.5 %collective-permute-start = (f32[512,512]{0,1:T(8,128)}, f32[512,512]{0,1:T(8,128)S(1)}, u32[]{:S(2)}, u32[]{:S(2)}) collective-permute-start(f32[512,512]{0,1:T(8,128)} %fusion.27), channel_id=1, source_target_pairs={{4,0},{8,4},{12,8},{16,12},{20,16},{24,20},{28,24},{5,1},{9,5},{13... | collective-permute-start | bytes 3145736 | tf_op jit(solution)/shard_map/while/body/eval_jaxpr/ppermute | solution.py:12
  179.8 3.5 %copy-start.2 = (f32[512,512]{0,1:T(8,128)S(1)}, f32[512,512]{0,1:T(8,128)}, u32[]{:S(2)}) copy-start(f32[512,512]{0,1:T(8,128)} %get-tuple-element.73) | copy-start | bytes 3145732 | tf_op jit(solution)/shard_map/while
  187.7 23.6 %collective-permute-start = (f32[512,512]{0,1:T(8,128)}, f32[512,512]{0,1:T(8,128)S(1)}, u32[]{:S(2)}, u32[]{:S(2)}) collective-permute-start(f32[512,512]{0,1:T(8,128)} %fusion.27), channel_id=1, source_target_pairs={{4,0},{8,4},{12,8},{16,12},{20,16},{24,20},{28,24},{5,1},{9,5},{13... | collective-permute-start | bytes 3145736 | tf_op jit(solution)/shard_map/while/body/eval_jaxpr/ppermute | solution.py:12
  211.3 3.5 %copy-start.2 = (f32[512,512]{0,1:T(8,128)S(1)}, f32[512,512]{0,1:T(8,128)}, u32[]{:S(2)}) copy-start(f32[512,512]{0,1:T(8,128)} %get-tuple-element.73) | copy-start | bytes 3145732 | tf_op jit(solution)/shard_map/while
  219.3 22.8 %collective-permute-start = (f32[512,512]{0,1:T(8,128)}, f32[512,512]{0,1:T(8,128)S(1)}, u32[]{:S(2)}, u32[]{:S(2)}) collective-permute-start(f32[512,512]{0,1:T(8,128)} %fusion.27), channel_id=1, source_target_pairs={{4,0},{8,4},{12,8},{16,12},{20,16},{24,20},{28,24},{5,1},{9,5},{13... | collective-permute-start | bytes 3145736 | tf_op jit(solution)/shard_map/while/body/eval_jaxpr/ppermute | solution.py:12
  242.0 4.5 %copy-start.3 = (f32[512,512]{0,1:T(8,128)S(1)}, f32[512,512]{0,1:T(8,128)}, u32[]{:S(2)}) copy-start(f32[512,512]{0,1:T(8,128)} %get-tuple-element.78) | copy-start | bytes 3145732
  245.5 1.0 copy-start.4
Sparse Core Ops, SparseCore 0:
  254.2 78.8 all-reduce.1
where the time goes:
time: 346 us; the launch traced here: 342 us
  waiting for transfers between devices  220 us (64%)
  matrix products  66.4 us (19%)
  starting transfers between devices  33.3 us (10%)
  between operations  14.1 us (4%)
  local copies, waits for them, and re-layouts  6.14 us (2%)
    ppermute x7, waiting for transfers between devices, passed_along(): return lax.ppermute(block, axis, route)  142 us
    psum x1, waiting for transfers between devices, on_device(): gradient = lax.psum(accumulated, 'tm') / (total_blocks - 1)  77.7 us
    dot_general x9, matrix products, product(): jnp.dot(left, right, precision=highest, preferred_element_type=jnp.float32)  38.7 us
    ppermute x7, starting transfers between devices, passed_along(): return lax.ppermute(block, axis, route)  33.3 us
    dot_general x8, matrix products, times_transposed(): lax.dot_general(left, right, (((1,), (1,)), ((), ())), precision=highest,...  27.8 us
  transfers between devices with their start and end apart: 8, of which 8 were waited for; matrix products, arithmetic and copies ran while one was open for 0% of the time, Pallas kernels for 0%

commit v1 on v0

v1 whole, which is shorter than its diff:
```python
import functools

import jax
import jax.numpy as jnp
from jax import lax
from jax.experimental import pallas as pl
from jax.experimental.pallas import tpu as pltpu
from jax.sharding import PartitionSpec as P

CHUNKS = 4


def split(value):
    high = value.astype(jnp.bfloat16)
    low = (value - high.astype(jnp.float32)).astype(jnp.bfloat16)
    return high, low


def product(left, right, transposed=False):
    dims = (((1,), (1 if transposed else 0,)), ((), ()))

    def dot(a, b):
        return lax.dot_general(a, b, dims, preferred_element_type=jnp.float32)

    return dot(left[0], right[0]) + (dot(left[0], right[1]) + dot(left[1], right[0]))


def kernel(
    n, g_ref, c_ref, f_ref, cov_ref, grad_ref,
    g_in, c_in, c_odd, cov_in, grad_buf, sum_in, sum_out, d_half, k_half, s_half,
    ge, go, a, f, e, l_half,
    pair_send, pair_recv, down_send, down_recv, side_send, side_recv,
    sum_send, sum_recv, up_send, up_recv, share_send, share_recv,
):
    width = f_ref.shape[0]
    half = width // 2
    rows = width // CHUNKS
    me = lax.axis_index("tm")
    side, pair, pairs = me % 2, me // 2, n // 2
    is_even, is_odd = side == 0, side == 1
    partner, up, down = me + 1 - 2 * side, me + 2, me - 2
    has_up, has_down = pair < pairs - 1, pair > 0
    mine = pl.ds(pl.multiple_of(side * half, half), half)
    other = pl.ds(pl.multiple_of((1 - side) * half, half), half)

    def chunk(r):
        return pl.ds(r * rows, rows)

    def remote(src, dst, send, recv, device):
        return pltpu.make_async_remote_copy(
            src_ref=src, dst_ref=dst, send_sem=send, recv_sem=recv,
            device_id={"tm": device}, device_id_type=pl.DeviceIdType.MESH,
        )

    def get(pair_ref, *index):
        return pair_ref[(0, *index)], pair_ref[(1, *index)]

    def put(pair_ref, value, *index):
        high, low = split(value)
        pair_ref[(0, *index)] = high
        pair_ref[(1, *index)] = low

    every = slice(None)

    barrier = pltpu.get_barrier_semaphore()

    def greet(device):
        pl.semaphore_signal(
            barrier, inc=1, device_id={"tm": device}, device_id_type=pl.DeviceIdType.MESH
        )

    greet(partner)
    pl.when(has_up)(lambda: greet(up))
    pl.when(has_down)(lambda: greet(down))
    pl.semaphore_wait(barrier, 1 + has_up.astype(jnp.int32) + has_down.astype(jnp.int32))

    send_g = remote(g_ref.at[0], g_in, pair_send.at[0], pair_recv.at[0], partner)
    send_c = remote(c_ref.at[0], c_in, pair_send.at[1], pair_recv.at[1], partner)
    send_c_half = remote(
        c_ref.at[0, :, pl.ds(half, half)], c_in.at[:, pl.ds(half, half)],
        pair_send.at[1], pair_recv.at[1], partner,
    )

    @pl.when(is_odd)
    def _():
        send_c.start()
        send_g.start()

    @pl.when(is_even)
    def _():
        send_g.start()
        send_c_half.start()

    put(f, f_ref[...], every, every)

    @pl.when(is_even)
    def _():
        put(ge, g_ref[0], every, every)
        send_c.wait_recv()
        c_odd[...] = c_in[...]

    @pl.when(is_odd)
    def _():
        c_odd[...] = c_ref[0]
        put(go, g_ref[0], every, every)
        send_g.wait_recv()
        put(ge, g_in[...], every, every)

    k_value = product(split(c_odd[...]), get(ge, mine, every), True)
    k_half[...] = k_value
    d_half[...] = product(get(ge, every, every), split(k_value))

    @pl.when(is_even)
    def _():
        d_half[...] += c_ref[0, :, :half]

    @pl.when(is_odd)
    def _():
        send_c_half.wait_recv()
        d_half[...] += c_in[:, half:]

    def send_down(r):
        return remote(
            s_half.at[chunk(r)], cov_in.at[side, chunk(r)], down_send.at[r], down_recv.at[r], down
        )

    def send_side(r):
        return remote(
            cov_in.at[side, chunk(r)], cov_in.at[side, chunk(r)],
            side_send.at[r], side_recv.at[r], partner,
        )

    @pl.when(jnp.logical_not(has_up))
    def _():
        s_half[...] = d_half[...]
        for r in range(CHUNKS):
            pl.when(has_down)(send_down(r).start)

    @pl.when(is_even)
    def _():
        send_g.wait_recv()
        put(go, g_in[...], every, every)

    @pl.when(jnp.logical_not(has_up))
    def _():
        e[...] = jnp.zeros_like(e)
        l_half[...] = jnp.zeros_like(l_half)

    @pl.when(has_up)
    def _():
        put(a, product(get(ge, every, every), get(go, every, every)), every, every)
        for r in range(CHUNKS + 1):
            if r < CHUNKS:
                send_down(r).wait_recv()
                send_side(r).start()
            if r > 0:
                q = chunk(r - 1)
                send_side(r - 1).wait_recv()
                put(e, cov_in[0, q], q, slice(0, half))
                put(e, cov_in[1, q], q, slice(half, width))
                put(l_half, product(get(e, q, every), get(a, mine, every), True), q, every)
        for r in range(CHUNKS):
            q = chunk(r)
            s_half[q] = product(get(a, q, every), get(l_half, every, every)) + d_half[q]
            pl.when(has_down)(send_down(r).start)

    lag_odd = product(get(e, every, every), get(go, mine, every), True)
    sigma_odd = product(get(go, every, every), split(lag_odd))

    @pl.when(is_even)
    def _():
        sum_out[...] = sigma_odd + c_odd[:, :half]

    @pl.when(is_odd)
    def _():
        own = sigma_odd + c_odd[:, half:]
        sum_out[...] = own
        cov_ref[0, :, half:] = own

    counted = jnp.where(has_up, 1.0, 0.0).astype(jnp.float32)
    variance = counted * sum_out[...] + s_half[...]
    terms = (
        lag_odd
        + (product(get(go, every, every), get(l_half, every, every)) + k_half[...])
        - product(get(f, every, every), split(variance))
    )
    send_sum = remote(sum_out, sum_in, sum_send, sum_recv, down)
    sum_out[...] = terms

    @pl.when(has_up)
    def _():
        send_sum.wait_recv()
        sum_out[...] += sum_in[...]

    pl.when(has_down)(send_sum.start)

    def send_up(r):
        return remote(
            grad_buf.at[side, chunk(r)], grad_buf.at[side, chunk(r)],
            up_send.at[r], up_recv.at[r], up,
        )

    def share(r):
        return remote(
            grad_buf.at[side, chunk(r)], grad_buf.at[side, chunk(r)],
            share_send.at[r], share_recv.at[r], partner,
        )

    @pl.when(jnp.logical_not(has_down))
    def _():
        grad_buf[side] = sum_out[...] / (n - 1)
        for r in range(CHUNKS):
            pl.when(has_up)(send_up(r).start)
            share(r).start()

    @pl.when(is_even)
    def _():
        cov_ref[0, :, :half] = s_half[...]
        k_other = product(split(c_odd[...]), get(ge, other, every), True)
        cov_ref[0, :, half:] = (
            product(get(ge, every, every), split(k_other)) + c_ref[0, :, half:]
        )

        @pl.when(has_up)
        def _():
            l_other = product(get(e, every, every), get(a, other, every), True)
            cov_ref[0, :, half:] += product(get(a, every, every), split(l_other))

    @pl.when(is_odd)
    def _():
        l_other = product(get(e, every, every), get(go, other, every), True)
        cov_ref[0, :, :half] = (
            product(get(go, every, every), split(l_other)) + c_odd[:, :half]
        )

    @pl.when(has_down)
    def _():
        for r in range(CHUNKS):
            send_up(r).wait_recv()
            pl.when(has_up)(send_up(r).start)
            share(r).start()

    for r in range(CHUNKS):
        share(r).wait_recv()
        grad_ref[chunk(r), :half] = grad_buf[0, chunk(r)]
        grad_ref[chunk(r), half:] = grad_buf[1, chunk(r)]

    send_g.wait_send()
    pl.when(is_odd)(send_c.wait_send)
    pl.when(is_even)(send_c_half.wait_send)
    pl.when(has_down)(send_sum.wait_send)
    for r in range(CHUNKS):
        pl.when(has_down)(send_down(r).wait_send)
        pl.when(has_up)(send_side(r).wait_send)
        pl.when(has_up)(send_up(r).wait_send)
        share(r).wait_send()


def on_device(n, transitions, cond_covs, transition_est):
    width = transitions.shape[1]
    half = width // 2
    f32, b16 = jnp.float32, jnp.bfloat16
    vmem = pl.BlockSpec(memory_space=pltpu.VMEM)
    whole, column_half = (width, width), (width, half)
    dma = pltpu.SemaphoreType.DMA
    return pl.pallas_call(
        functools.partial(kernel, n),
        out_shape=(
            jax.ShapeDtypeStruct(transitions.shape, f32),
            jax.ShapeDtypeStruct(transition_est.shape, f32),
        ),
        in_specs=[vmem] * 3,
        out_specs=(vmem, vmem),
        scratch_shapes=[
            pltpu.VMEM(whole, f32),
            pltpu.VMEM(whole, f32),
            pltpu.VMEM(whole, f32),
            pltpu.VMEM((2, *column_half), f32),
            pltpu.VMEM((2, *column_half), f32),
            pltpu.VMEM(column_half, f32),
            pltpu.VMEM(column_half, f32),
            pltpu.VMEM(column_half, f32),
            pltpu.VMEM(column_half, f32),
            pltpu.VMEM(column_half, f32),
            pltpu.VMEM((2, *whole), b16),
            pltpu.VMEM((2, *whole), b16),
            pltpu.VMEM((2, *whole), b16),
            pltpu.VMEM((2, *whole), b16),
            pltpu.VMEM((2, *whole), b16),
            pltpu.VMEM((2, *column_half), b16),
            dma((2,)), dma((2,)),
            dma((CHUNKS,)), dma((CHUNKS,)), dma((CHUNKS,)), dma((CHUNKS,)),
            dma, dma,
            dma((CHUNKS,)), dma((CHUNKS,)), dma((CHUNKS,)), dma((CHUNKS,)),
        ],
        compiler_params=pltpu.CompilerParams(
            collective_id=0, has_side_effects=True, vmem_limit_bytes=56 * 2**20
        ),
    )(transitions, cond_covs, transition_est)


def solution(mesh):
    return jax.shard_map(
        functools.partial(on_device, mesh.shape["tm"]),
        mesh=mesh,
        in_specs=(P(("rep", "tm"), None, None), P(("rep", "tm"), None, None), P("rep", None)),
        out_specs=(P(("rep", "tm"), None, None), P("rep", None)),
        check_vma=False,
    )
```

time: 346 us -> 133 us (0.38); the launches traced: 342 us -> 133 us
  waiting for transfers between devices: 220 us -> 0 us
  Pallas kernels: 0 us -> 129 us
  matrix products: 66.4 us -> 0 us
  starting transfers between devices: 33.3 us -> 0 us
  between operations: 14.1 us -> 0.65 us
    ppermute x7 -> x0, waiting for transfers between devices: 142 us -> none  [passed_along(): return lax.ppermute(block, axis, route)]
    pallas_call x0 -> x1, Pallas kernels: none -> 129 us  [on_device(): pl.pallas_call(functools.partial(kernel, n), out_shape=(jax.ShapeDtypeStr...]
    psum x1 -> x0, waiting for transfers between devices: 77.7 us -> none  [on_device(): gradient = lax.psum(accumulated, 'tm') / (total_blocks - 1)]
    dot_general x17 -> x0, matrix products: 66.4 us -> none  [the longest x9 38.7 us: product(): jnp.dot(left, right, precision=highest, preferred_element_type=jnp.float32)]
    ppermute x7 -> x0, starting transfers between devices: 33.3 us -> none  [passed_along(): return lax.ppermute(block, axis, route)]
  transfers between devices with their start and end apart: 8 -> 0, of which waited for: 8 -> 0; matrix products, arithmetic and copies ran while one was open for 0% -> 0% of each run, Pallas kernels for 0% -> 0%
where the time goes in v1:
time: 133 us
  Pallas kernels  129 us (97%)
  local copies, waits for them, and re-layouts  3.32 us (2%)
    pallas_call x1, Pallas kernels, on_device(): pl.pallas_call(functools.partial(kernel, n), out_shape=(jax.ShapeDtypeStr...  129 us
    unnamed x4, local copies, waits for them, and re-layouts  3.32 us

profile of v1, /device:TPU:26, one launch (start us, length us, event | category | flops | bytes accessed | tf_op | source)
XLA Modules:
  0.0 132.7 jit_solution(3237307030844173050)
XLA Ops:
  0.6 128.8 %shard_map.50 = (f32[1,512,512]{2,1,0:T(8,128)}, f32[512,512]{1,0:T(8,128)}) custom-call(f32[1,512,512]{2,1,0:T(8,128)} %g_ref.1, f32[1,512,512]{2,1,0:T(8,128)} %c_ref.1, f32[512,512]{1,0:T(8,128)} %f_ref.1), custom_call_target="tpu_custom_call" | custom-call | tf_op jit(solution)/shard_map/pallas_call | solution.py:266
  129.4 0.0 copy-start
  129.4 2.4 %copy.7 = f32[1,512,512]{2,1,0:T(8,128)} copy(f32[1,512,512]{2,1,0:T(8,128)} %get-tuple-element.4) | data formatting | bytes 2097152
  131.8 0.0 copy-done
  131.8 1.0 copy.8
Async XLA Ops:
  129.4 2.4 %copy-start = (f32[512,512]{1,0:T(8,128)S(1)}, f32[512,512]{1,0:T(8,128)}, u32[]{:S(2)}) copy-start(f32[512,512]{1,0:T(8,128)} %get-tuple-element.5) | copy-start | bytes 3145732

commit v2 on v1

--- a/solution.py
+++ b/solution.py
@@ -8,6 +8,7 @@
 from jax.sharding import PartitionSpec as P
 
 CHUNKS = 4
+PIECES = 2
 
 
 def split(value):
@@ -28,7 +29,7 @@
 def kernel(
     n, g_ref, c_ref, f_ref, cov_ref, grad_ref,
     g_in, c_in, c_odd, cov_in, grad_buf, sum_in, sum_out, d_half, k_half, s_half,
-    ge, go, a, f, e, l_half,
+    lag_odd, sigma_odd, ge, go, a, f, e, l_half, v_half,
     pair_send, pair_recv, down_send, down_recv, side_send, side_recv,
     sum_send, sum_recv, up_send, up_recv, share_send, share_recv,
 ):
@@ -46,6 +47,14 @@
     def chunk(r):
         return pl.ds(r * rows, rows)
 
+    sends = CHUNKS * PIECES
+
+    def piece(t):
+        return pl.ds(t * (width // sends), width // sends)
+
+    def pieces(r):
+        return range(r * PIECES, (r + 1) * PIECES)
+
     def remote(src, dst, send, recv, device):
         return pltpu.make_async_remote_copy(
             src_ref=src, dst_ref=dst, send_sem=send, recv_sem=recv,
@@ -121,19 +130,19 @@
 
     def send_down(r):
         return remote(
-            s_half.at[chunk(r)], cov_in.at[side, chunk(r)], down_send.at[r], down_recv.at[r], down
+            s_half.at[piece(r)], cov_in.at[side, piece(r)], down_send.at[r], down_recv.at[r], down
         )
 
     def send_side(r):
         return remote(
-            cov_in.at[side, chunk(r)], cov_in.at[side, chunk(r)],
+            cov_in.at[side, piece(r)], cov_in.at[side, piece(r)],
             side_send.at[r], side_recv.at[r], partner,
         )
 
     @pl.when(jnp.logical_not(has_up))
     def _():
         s_half[...] = d_half[...]
-        for r in range(CHUNKS):
+        for r in range(sends):
             pl.when(has_down)(send_down(r).start)
 
     @pl.when(is_even)
@@ -145,73 +154,83 @@
     def _():
         e[...] = jnp.zeros_like(e)
         l_half[...] = jnp.zeros_like(l_half)
+        lag_odd[...] = jnp.zeros_like(lag_odd)
 
     @pl.when(has_up)
     def _():
         put(a, product(get(ge, every, every), get(go, every, every)), every, every)
-        for r in range(CHUNKS + 1):
-            if r < CHUNKS:
-                send_down(r).wait_recv()
-                send_side(r).start()
-            if r > 0:
-                q = chunk(r - 1)
-                send_side(r - 1).wait_recv()
-                put(e, cov_in[0, q], q, slice(0, half))
-                put(e, cov_in[1, q], q, slice(half, width))
-                put(l_half, product(get(e, q, every), get(a, mine, every), True), q, every)
+        for t in range(sends + 1):
+            if t < sends:
+                send_down(t).wait_recv()
+                send_side(t).start()
+            if t > 0:
+                send_side(t - 1).wait_recv()
+                if t % PIECES == 0:
+                    q = chunk(t // PIECES - 1)
+                    put(e, cov_in[0, q], q, slice(0, half))
+                    put(e, cov_in[1, q], q, slice(half, width))
+                    rows_of_e = get(e, q, every)
+                    put(l_half, product(rows_of_e, get(a, mine, every), True), q, every)
+                    lag_odd[q] = product(rows_of_e, get(go, mine, every), True)
         for r in range(CHUNKS):
             q = chunk(r)
             s_half[q] = product(get(a, q, every), get(l_half, every, every)) + d_half[q]
-            pl.when(has_down)(send_down(r).start)
-
-    lag_odd = product(get(e, every, every), get(go, mine, every), True)
-    sigma_odd = product(get(go, every, every), split(lag_odd))
-
-    @pl.when(is_even)
-    def _():
-        sum_out[...] = sigma_odd + c_odd[:, :half]
-
-    @pl.when(is_odd)
-    def _():
-        own = sigma_odd + c_odd[:, half:]
-        sum_out[...] = own
+            for t in pieces(r):
+                pl.when(has_down)(send_down(t).start)
+
+    sigma_odd[...] = product(get(go, every, every), split(lag_odd[...]))
+
+    @pl.when(is_even)
+    def _():
+        sigma_odd[...] += c_odd[:, :half]
+
+    @pl.when(is_odd)
+    def _():
+        own = sigma_odd[...] + c_odd[:, half:]
+        sigma_odd[...] = own
         cov_ref[0, :, half:] = own
 
     counted = jnp.where(has_up, 1.0, 0.0).astype(jnp.float32)
-    variance = counted * sum_out[...] + s_half[...]
-    terms = (
-        lag_odd
-        + (product(get(go, every, every), get(l_half, every, every)) + k_half[...])
-        - product(get(f, every, every), split(variance))
-    )
-    send_sum = remote(sum_out, sum_in, sum_send, sum_recv, down)
-    sum_out[...] = terms
-
-    @pl.when(has_up)
-    def _():
-        send_sum.wait_recv()
-        sum_out[...] += sum_in[...]
-
-    pl.when(has_down)(send_sum.start)
+    put(v_half, counted * sigma_odd[...] + s_half[...], every, every)
+
+    def send_sum(r):
+        return remote(
+            sum_out.at[chunk(r)], sum_in.at[chunk(r)], sum_send.at[r], sum_recv.at[r], down
+        )
 
     def send_up(r):
         return remote(
-            grad_buf.at[side, chunk(r)], grad_buf.at[side, chunk(r)],
+            grad_buf.at[side, piece(r)], grad_buf.at[side, piece(r)],
             up_send.at[r], up_recv.at[r], up,
         )
 
     def share(r):
         return remote(
-            grad_buf.at[side, chunk(r)], grad_buf.at[side, chunk(r)],
+            grad_buf.at[side, piece(r)], grad_buf.at[side, piece(r)],
             share_send.at[r], share_recv.at[r], partner,
         )
 
-    @pl.when(jnp.logical_not(has_down))
-    def _():
-        grad_buf[side] = sum_out[...] / (n - 1)
-        for r in range(CHUNKS):
-            pl.when(has_up)(send_up(r).start)
-            share(r).start()
+    for r in range(CHUNKS):
+        q = chunk(r)
+        sum_out[q] = (
+            lag_odd[q]
+            + (product(get(go, q, every), get(l_half, every, every)) + k_half[q])
+            - product(get(f, q, every), get(v_half, every, every))
+        )
+
+        @pl.when(has_up)
+        def _():
+            send_sum(r).wait_recv()
+            sum_out[q] += sum_in[q]
+
+        pl.when(has_down)(send_sum(r).start)
+
+        @pl.when(jnp.logical_not(has_down))
+        def _():
+            grad_buf[side, q] = sum_out[q] / (n - 1)
+            for t in pieces(r):
+                pl.when(has_up)(send_up(t).start)
+                share(t).start()
 
     @pl.when(is_even)
     def _():
@@ -235,21 +254,22 @@
 
     @pl.when(has_down)
     def _():
-        for r in range(CHUNKS):
+        for r in range(sends):
             send_up(r).wait_recv()
             pl.when(has_up)(send_up(r).start)
             share(r).start()
 
-    for r in range(CHUNKS):
+    for r in range(sends):
         share(r).wait_recv()
-        grad_ref[chunk(r), :half] = grad_buf[0, chunk(r)]
-        grad_ref[chunk(r), half:] = grad_buf[1, chunk(r)]
+        grad_ref[piece(r), :half] = grad_buf[0, piece(r)]
+        grad_ref[piece(r), half:] = grad_buf[1, piece(r)]
 
     send_g.wait_send()
     pl.when(is_odd)(send_c.wait_send)
     pl.when(is_even)(send_c_half.wait_send)
-    pl.when(has_down)(send_sum.wait_send)
     for r in range(CHUNKS):
+        pl.when(has_down)(send_sum(r).wait_send)
+    for r in range(sends):
         pl.when(has_down)(send_down(r).wait_send)
         pl.when(has_up)(send_side(r).wait_send)
         pl.when(has_up)(send_up(r).wait_send)
@@ -263,6 +283,7 @@
     vmem = pl.BlockSpec(memory_space=pltpu.VMEM)
     whole, column_half = (width, width), (width, half)
     dma = pltpu.SemaphoreType.DMA
+    sends = CHUNKS * PIECES
     return pl.pallas_call(
         functools.partial(kernel, n),
         out_shape=(
@@ -272,26 +293,15 @@
         in_specs=[vmem] * 3,
         out_specs=(vmem, vmem),
         scratch_shapes=[
-            pltpu.VMEM(whole, f32),
-            pltpu.VMEM(whole, f32),
-            pltpu.VMEM(whole, f32),
-            pltpu.VMEM((2, *column_half), f32),
-            pltpu.VMEM((2, *column_half), f32),
-            pltpu.VMEM(column_half, f32),
-            pltpu.VMEM(column_half, f32),
-            pltpu.VMEM(column_half, f32),
-            pltpu.VMEM(column_half, f32),
-            pltpu.VMEM(column_half, f32),
-            pltpu.VMEM((2, *whole), b16),
-            pltpu.VMEM((2, *whole), b16),
-            pltpu.VMEM((2, *whole), b16),
-            pltpu.VMEM((2, *whole), b16),
-            pltpu.VMEM((2, *whole), b16),
-            pltpu.VMEM((2, *column_half), b16),
-            dma((2,)), dma((2,)),
-            dma((CHUNKS,)), dma((CHUNKS,)), dma((CHUNKS,)), dma((CHUNKS,)),
-            dma, dma,
-            dma((CHUNKS,)), dma((CHUNKS,)), dma((CHUNKS,)), dma((CHUNKS,)),
+            *[pltpu.VMEM(whole, f32)] * 3,
+            *[pltpu.VMEM((2, *column_half), f32)] * 2,
+            *[pltpu.VMEM(column_half, f32)] * 7,
+            *[pltpu.VMEM((2, *whole), b16)] * 5,
+            *[pltpu.VMEM((2, *column_half), b16)] * 2,
+            *[dma((2,))] * 2,
+            *[dma((sends,))] * 4,
+            *[dma((CHUNKS,))] * 2,
+            *[dma((sends,))] * 4,
         ],
         compiler_params=pltpu.CompilerParams(
             collective_id=0, has_side_effects=True, vmem_limit_bytes=56 * 2**20

time: 133 us -> 139 us (1.045)
  Pallas kernels: 129 us -> 134 us
    pallas_call x1, Pallas kernels: 129 us -> 134 us  [on_device(): pl.pallas_call(functools.partial(kernel, n), out_shape=(jax.ShapeDtypeStr...]
where the time goes in v2:
time: 139 us; the launch traced here: 138 us
  Pallas kernels  134 us (96%)
  local copies, waits for them, and re-layouts  3.32 us (2%)
    pallas_call x1, Pallas kernels, on_device(): pl.pallas_call(functools.partial(kernel, n), out_shape=(jax.ShapeDtypeStr...  134 us
    unnamed x4, local copies, waits for them, and re-layouts  3.32 us

profile of v2, /device:TPU:26, one launch (start us, length us, event | category | flops | bytes accessed | tf_op | source)
XLA Modules:
  0.0 138.4 jit_solution(16622539652027383819)
XLA Ops:
  0.6 134.4 %shard_map.50 = (f32[1,512,512]{2,1,0:T(8,128)}, f32[512,512]{1,0:T(8,128)}) custom-call(f32[1,512,512]{2,1,0:T(8,128)} %g_ref.1, f32[1,512,512]{2,1,0:T(8,128)} %c_ref.1, f32[512,512]{1,0:T(8,128)} %f_ref.1), custom_call_target="tpu_custom_call" | custom-call | tf_op jit(solution)/shard_map/pallas_call | solution.py:287
  135.0 0.0 copy-start
  135.0 2.4 %copy.7 = f32[1,512,512]{2,1,0:T(8,128)} copy(f32[1,512,512]{2,1,0:T(8,128)} %get-tuple-element.4) | data formatting | bytes 2097152
  137.4 0.0 copy-done
  137.4 1.0 copy.8
Async XLA Ops:
  135.0 2.4 %copy-start = (f32[512,512]{1,0:T(8,128)S(1)}, f32[512,512]{1,0:T(8,128)}, u32[]{:S(2)}) copy-start(f32[512,512]{1,0:T(8,128)} %get-tuple-element.5) | copy-start | bytes 3145732

commit v3 on v2

--- a/solution.py
+++ b/solution.py
@@ -30,7 +30,7 @@
     n, g_ref, c_ref, f_ref, cov_ref, grad_ref,
     g_in, c_in, c_odd, cov_in, grad_buf, sum_in, sum_out, d_half, k_half, s_half,
     lag_odd, sigma_odd, ge, go, a, f, e, l_half, v_half,
-    pair_send, pair_recv, down_send, down_recv, side_send, side_recv,
+    pair_send, pair_recv, top_send, top_recv, down_send, down_recv, side_send, side_recv,
     sum_send, sum_recv, up_send, up_recv, share_send, share_recv,
 ):
     width = f_ref.shape[0]
@@ -83,100 +83,163 @@
     pl.when(has_down)(lambda: greet(down))
     pl.semaphore_wait(barrier, 1 + has_up.astype(jnp.int32) + has_down.astype(jnp.int32))
 
+    is_top = jnp.logical_not(has_up)
+    low, high = pl.ds(0, half), pl.ds(half, half)
+
+    def swap(i, ref, target, *index):
+        return remote(
+            ref.at[(0, *index)], target.at[index], pair_send.at[i], pair_recv.at[i], partner
+        )
+
     send_g = remote(g_ref.at[0], g_in, pair_send.at[0], pair_recv.at[0], partner)
-    send_c = remote(c_ref.at[0], c_in, pair_send.at[1], pair_recv.at[1], partner)
-    send_c_half = remote(
-        c_ref.at[0, :, pl.ds(half, half)], c_in.at[:, pl.ds(half, half)],
-        pair_send.at[1], pair_recv.at[1], partner,
-    )
+    send_c_low = swap(1, c_ref, c_in, low)
+    send_c_high = swap(2, c_ref, c_in, high, high)
+    send_c_half = swap(1, c_ref, c_in, every, high)
 
     @pl.when(is_odd)
     def _():
-        send_c.start()
-        send_g.start()
-
-    @pl.when(is_even)
+        pl.when(has_up)(send_g.start)
+        send_c_low.start()
+        send_c_high.start()
+
+    @pl.when(is_even & has_up)
     def _():
         send_g.start()
         send_c_half.start()
 
+    def receive_c_odd():
+        send_c_low.wait_recv()
+        send_c_high.wait_recv()
+        c_odd[low] = c_in[low]
+        c_odd[high, half:] = c_in[high, half:]
+        c_odd[high, :half] = c_in[low, half:].T
+
+    def send_down(t):
+        return remote(
+            s_half.at[piece(t)], cov_in.at[side, piece(t)], down_send.at[t], down_recv.at[t], down
+        )
+
+    def send_side(t):
+        return remote(
+            cov_in.at[side, piece(t)], cov_in.at[side, piece(t)],
+            side_send.at[t], side_recv.at[t], partner,
+        )
+
+    forwards = is_even | (pair < pairs - 2)
+
+    def send_top(t):
+        return remote(
+            d_half.at[piece(t)], s_half.at[piece(t)], top_send.at[t], top_recv.at[t], partner
+        )
+
+    def send_other_down(t):
+        return remote(
+            d_half.at[piece(t)], cov_in.at[1, piece(t)], side_send.at[t], side_recv.at[t], down
+        )
+
+    @pl.when(is_even)
+    def _():
+        put(ge, g_ref[0], every, every)
+
+    @pl.when(is_odd)
+    def _():
+        c_odd[...] = c_ref[0]
+
+    @pl.when(is_top)
+    def _():
+        e[...] = jnp.zeros_like(e)
+        go[...] = jnp.zeros_like(go)
+        l_half[...] = jnp.zeros_like(l_half)
+        lag_odd[...] = jnp.zeros_like(lag_odd)
+
+    @pl.when(is_top & is_even)
+    def _():
+        receive_c_odd()
+        k_all = product(split(c_odd[...]), get(ge, every, every), True)
+        k_half[...] = k_all[:, :half]
+        put(e, k_all, every, every)
+        for r in range(CHUNKS):
+            q = chunk(r)
+            sigma = product(get(ge, q, every), get(e, every, every)) + c_ref[0, q]
+            s_half[q] = sigma[:, :half]
+            d_half[q] = sigma[:, half:]
+            for t in pieces(r):
+                send_top(t).start()
+                pl.when(has_down)(send_down(t).start)
+                pl.when(has_down)(send_other_down(t).start)
+        send_g.start()
+        e[...] = jnp.zeros_like(e)
+
     put(f, f_ref[...], every, every)
 
-    @pl.when(is_even)
-    def _():
-        put(ge, g_ref[0], every, every)
-        send_c.wait_recv()
-        c_odd[...] = c_in[...]
-
-    @pl.when(is_odd)
-    def _():
-        c_odd[...] = c_ref[0]
-        put(go, g_ref[0], every, every)
+    @pl.when(is_top & is_odd)
+    def _():
+        for t in range(sends):
+            send_top(t).wait_recv()
+            pl.when(has_down)(send_down(t).start)
         send_g.wait_recv()
         put(ge, g_in[...], every, every)
-
-    k_value = product(split(c_odd[...]), get(ge, mine, every), True)
-    k_half[...] = k_value
-    d_half[...] = product(get(ge, every, every), split(k_value))
-
-    @pl.when(is_even)
-    def _():
-        d_half[...] += c_ref[0, :, :half]
-
-    @pl.when(is_odd)
-    def _():
-        send_c_half.wait_recv()
-        d_half[...] += c_in[:, half:]
-
-    def send_down(r):
-        return remote(
-            s_half.at[piece(r)], cov_in.at[side, piece(r)], down_send.at[r], down_recv.at[r], down
-        )
-
-    def send_side(r):
-        return remote(
-            cov_in.at[side, piece(r)], cov_in.at[side, piece(r)],
-            side_send.at[r], side_recv.at[r], partner,
-        )
-
-    @pl.when(jnp.logical_not(has_up))
-    def _():
-        s_half[...] = d_half[...]
-        for r in range(sends):
-            pl.when(has_down)(send_down(r).start)
-
-    @pl.when(is_even)
-    def _():
-        send_g.wait_recv()
-        put(go, g_in[...], every, every)
-
-    @pl.when(jnp.logical_not(has_up))
-    def _():
-        e[...] = jnp.zeros_like(e)
-        l_half[...] = jnp.zeros_like(l_half)
-        lag_odd[...] = jnp.zeros_like(lag_odd)
+        k_half[...] = product(split(c_odd[...]), get(ge, mine, every), True)
 
     @pl.when(has_up)
     def _():
+        @pl.when(is_even)
+        def _():
+            send_g.wait_recv()
+            put(go, g_in[...], every, every)
+
+        @pl.when(is_odd)
+        def _():
+            put(go, g_ref[0], every, every)
+            send_g.wait_recv()
+            put(ge, g_in[...], every, every)
+
         put(a, product(get(ge, every, every), get(go, every, every)), every, every)
-        for t in range(sends + 1):
-            if t < sends:
-                send_down(t).wait_recv()
-                send_side(t).start()
-            if t > 0:
-                send_side(t - 1).wait_recv()
-                if t % PIECES == 0:
-                    q = chunk(t // PIECES - 1)
-                    put(e, cov_in[0, q], q, slice(0, half))
-                    put(e, cov_in[1, q], q, slice(half, width))
-                    rows_of_e = get(e, q, every)
-                    put(l_half, product(rows_of_e, get(a, mine, every), True), q, every)
-                    lag_odd[q] = product(rows_of_e, get(go, mine, every), True)
+        pl.when(is_even)(receive_c_odd)
+        k_value = product(split(c_odd[...]), get(ge, mine, every), True)
+        k_half[...] = k_value
+        d_half[...] = product(get(ge, every, every), split(k_value))
+
+        @pl.when(is_even)
+        def _():
+            d_half[...] += c_ref[0, :, :half]
+
+        @pl.when(is_odd)
+        def _():
+            send_c_half.wait_recv()
+            d_half[...] += c_in[:, half:]
+
+        def use(r):
+            q = chunk(r)
+            for t in pieces(r):
+                send_side(t).wait_recv()
+            put(e, cov_in[0, q], q, slice(0, half))
+            put(e, cov_in[1, q], q, slice(half, width))
+            rows_of_e = get(e, q, every)
+            put(l_half, product(rows_of_e, get(a, mine, every), True), q, every)
+
+            @pl.when(jnp.logical_not(has_down))
+            def _():
+                lag_odd[q] = product(rows_of_e, get(go, mine, every), True)
+
+        used = 0
+        for t in range(sends):
+            send_down(t).wait_recv()
+            pl.when(forwards)(send_side(t).start)
+            if t % PIECES == 0 and t >= 2 * PIECES:
+                use(used)
+                used += 1
+        for r in range(used, CHUNKS):
+            use(r)
         for r in range(CHUNKS):
             q = chunk(r)
             s_half[q] = product(get(a, q, every), get(l_half, every, every)) + d_half[q]
             for t in pieces(r):
                 pl.when(has_down)(send_down(t).start)
+
+        @pl.when(has_down)
+        def _():
+            lag_odd[...] = product(get(e, every, every), get(go, mine, every), True)
 
     sigma_odd[...] = product(get(go, every, every), split(lag_odd[...]))
 
@@ -264,14 +327,17 @@
         grad_ref[piece(r), :half] = grad_buf[0, piece(r)]
         grad_ref[piece(r), half:] = grad_buf[1, piece(r)]
 
-    send_g.wait_send()
-    pl.when(is_odd)(send_c.wait_send)
-    pl.when(is_even)(send_c_half.wait_send)
+    pl.when(has_up | is_even)(send_g.wait_send)
+    pl.when(is_odd)(send_c_low.wait_send)
+    pl.when(is_odd)(send_c_high.wait_send)
+    pl.when(has_up & is_even)(send_c_half.wait_send)
     for r in range(CHUNKS):
         pl.when(has_down)(send_sum(r).wait_send)
     for r in range(sends):
         pl.when(has_down)(send_down(r).wait_send)
-        pl.when(has_up)(send_side(r).wait_send)
+        pl.when(has_up & forwards)(send_side(r).wait_send)
+        pl.when(is_top & is_even)(send_top(r).wait_send)
+        pl.when(is_top & is_even & has_down)(send_other_down(r).wait_send)
         pl.when(has_up)(send_up(r).wait_send)
         share(r).wait_send()
 
@@ -298,8 +364,8 @@
             *[pltpu.VMEM(column_half, f32)] * 7,
             *[pltpu.VMEM((2, *whole), b16)] * 5,
             *[pltpu.VMEM((2, *column_half), b16)] * 2,
-            *[dma((2,))] * 2,
-            *[dma((sends,))] * 4,
+            *[dma((3,))] * 2,
+            *[dma((sends,))] * 6,
             *[dma((CHUNKS,))] * 2,
             *[dma((sends,))] * 4,
         ],

time: 139 us -> 123 us (0.88)
  Pallas kernels: 134 us -> 118 us
    pallas_call x1, Pallas kernels: 134 us -> 118 us  [on_device(): pl.pallas_call(functools.partial(kernel, n), out_shape=(jax.ShapeDtypeStr...]
where the time goes in v3:
time: 123 us; the launch traced here: 122 us
  Pallas kernels  118 us (96%)
  local copies, waits for them, and re-layouts  3.32 us (3%)
    pallas_call x1, Pallas kernels, on_device(): pl.pallas_call(functools.partial(kernel, n), out_shape=(jax.ShapeDtypeStr...  118 us
    unnamed x4, local copies, waits for them, and re-layouts  3.32 us

profile of v3, /device:TPU:26, one launch (start us, length us, event | category | flops | bytes accessed | tf_op | source)
XLA Modules:
  0.0 122.4 jit_solution(18220820280678914611)
XLA Ops:
  0.6 118.5 %shard_map.50 = (f32[1,512,512]{2,1,0:T(8,128)}, f32[512,512]{1,0:T(8,128)}) custom-call(f32[1,512,512]{2,1,0:T(8,128)} %g_ref.1, f32[1,512,512]{2,1,0:T(8,128)} %c_ref.1, f32[512,512]{1,0:T(8,128)} %f_ref.1), custom_call_target="tpu_custom_call" | custom-call | tf_op jit(solution)/shard_map/pallas_call | solution.py:353
  119.1 0.0 copy-start
  119.1 2.4 %copy.7 = f32[1,512,512]{2,1,0:T(8,128)} copy(f32[1,512,512]{2,1,0:T(8,128)} %get-tuple-element.4) | data formatting | bytes 2097152
  121.4 0.0 copy-done
  121.5 1.0 copy.8
Async XLA Ops:
  119.1 2.4 %copy-start = (f32[512,512]{1,0:T(8,128)S(1)}, f32[512,512]{1,0:T(8,128)}, u32[]{:S(2)}) copy-start(f32[512,512]{1,0:T(8,128)} %get-tuple-element.5) | copy-start | bytes 3145732

commit v4 on v3

--- a/solution.py
+++ b/solution.py
@@ -8,7 +8,7 @@
 from jax.sharding import PartitionSpec as P
 
 CHUNKS = 4
-PIECES = 2
+PIECES = 4
 
 
 def split(value):
@@ -30,7 +30,7 @@
     n, g_ref, c_ref, f_ref, cov_ref, grad_ref,
     g_in, c_in, c_odd, cov_in, grad_buf, sum_in, sum_out, d_half, k_half, s_half,
     lag_odd, sigma_odd, ge, go, a, f, e, l_half, v_half,
-    pair_send, pair_recv, top_send, top_recv, down_send, down_recv, side_send, side_recv,
+    pair_send, pair_recv, top_send, top_recv, late_send, late_recv, down_send, down_recv, side_send, side_recv,
     sum_send, sum_recv, up_send, up_recv, share_send, share_recv,
 ):
     width = f_ref.shape[0]
@@ -125,7 +125,18 @@
             side_send.at[t], side_recv.at[t], partner,
         )
 
-    forwards = is_even | (pair < pairs - 2)
+    second = pair == pairs - 2
+    late = range(sends // 2, sends)
+
+    def forwards(t):
+        if t in late:
+            return jnp.logical_not(second)
+        return is_even | jnp.logical_not(second)
+
+    def send_late(t):
+        return remote(
+            s_half.at[piece(t)], d_half.at[piece(t)], late_send.at[t], late_recv.at[t], partner
+        )
 
     def send_top(t):
         return remote(
@@ -134,7 +145,7 @@
 
     def send_other_down(t):
         return remote(
-            d_half.at[piece(t)], cov_in.at[1, piece(t)], side_send.at[t], side_recv.at[t], down
+            d_half.at[piece(t)], cov_in.at[1 - side, piece(t)], side_send.at[t], side_recv.at[t], down
         )
 
     @pl.when(is_even)
@@ -165,6 +176,8 @@
             d_half[q] = sigma[:, half:]
             for t in pieces(r):
                 send_top(t).start()
+                if t in late:
+                    send_late(t).start()
                 pl.when(has_down)(send_down(t).start)
                 pl.when(has_down)(send_other_down(t).start)
         send_g.start()
@@ -177,6 +190,9 @@
         for t in range(sends):
             send_top(t).wait_recv()
             pl.when(has_down)(send_down(t).start)
+            if t in late:
+                send_late(t).wait_recv()
+                pl.when(has_down)(send_other_down(t).start)
         send_g.wait_recv()
         put(ge, g_in[...], every, every)
         k_half[...] = product(split(c_odd[...]), get(ge, mine, every), True)
@@ -225,7 +241,7 @@
         used = 0
         for t in range(sends):
             send_down(t).wait_recv()
-            pl.when(forwards)(send_side(t).start)
+            pl.when(forwards(t))(send_side(t).start)
             if t % PIECES == 0 and t >= 2 * PIECES:
                 use(used)
                 used += 1
@@ -335,9 +351,12 @@
         pl.when(has_down)(send_sum(r).wait_send)
     for r in range(sends):
         pl.when(has_down)(send_down(r).wait_send)
-        pl.when(has_up & forwards)(send_side(r).wait_send)
+        pl.when(has_up & forwards(r))(send_side(r).wait_send)
         pl.when(is_top & is_even)(send_top(r).wait_send)
         pl.when(is_top & is_even & has_down)(send_other_down(r).wait_send)
+        if r in late:
+            pl.when(is_top & is_even)(send_late(r).wait_send)
+            pl.when(is_top & is_odd & has_down)(send_other_down(r).wait_send)
         pl.when(has_up)(send_up(r).wait_send)
         share(r).wait_send()
 
@@ -365,7 +384,7 @@
             *[pltpu.VMEM((2, *whole), b16)] * 5,
             *[pltpu.VMEM((2, *column_half), b16)] * 2,
             *[dma((3,))] * 2,
-            *[dma((sends,))] * 6,
+            *[dma((sends,))] * 8,
             *[dma((CHUNKS,))] * 2,
             *[dma((sends,))] * 4,
         ],

time: 123 us -> 115 us (0.935)
  Pallas kernels: 118 us -> 110 us
    pallas_call x1, Pallas kernels: 118 us -> 110 us  [on_device(): pl.pallas_call(functools.partial(kernel, n), out_shape=(jax.ShapeDtypeStr...]
where the time goes in v4:
time: 115 us; the launch traced here: 114 us
  Pallas kernels  110 us (96%)
  local copies, waits for them, and re-layouts  3.32 us (3%)
    pallas_call x1, Pallas kernels, on_device(): pl.pallas_call(functools.partial(kernel, n), out_shape=(jax.ShapeDtypeStr...  110 us
    unnamed x4, local copies, waits for them, and re-layouts  3.32 us

profile of v4, /device:TPU:26, one launch (start us, length us, event | category | flops | bytes accessed | tf_op | source)
XLA Modules:
  0.0 114.4 jit_solution(8624729516664354840)
XLA Ops:
  0.6 110.5 %shard_map.50 = (f32[1,512,512]{2,1,0:T(8,128)}, f32[512,512]{1,0:T(8,128)}) custom-call(f32[1,512,512]{2,1,0:T(8,128)} %g_ref.1, f32[1,512,512]{2,1,0:T(8,128)} %c_ref.1, f32[512,512]{1,0:T(8,128)} %f_ref.1), custom_call_target="tpu_custom_call" | custom-call | tf_op jit(solution)/shard_map/pallas_call | solution.py:372
  111.1 0.0 copy-start
  111.1 2.4 %copy.7 = f32[1,512,512]{2,1,0:T(8,128)} copy(f32[1,512,512]{2,1,0:T(8,128)} %get-tuple-element.4) | data formatting | bytes 2097152
  113.5 0.0 copy-done
  113.5 1.0 copy.8
Async XLA Ops:
  111.1 2.4 %copy-start = (f32[512,512]{1,0:T(8,128)S(1)}, f32[512,512]{1,0:T(8,128)}, u32[]{:S(2)}) copy-start(f32[512,512]{1,0:T(8,128)} %get-tuple-element.5) | copy-start | bytes 3145732

commit v5 on v4

--- a/solution.py
+++ b/solution.py
@@ -127,6 +127,7 @@
 
     second = pair == pairs - 2
     late = range(sends // 2, sends)
+    ahead = second & is_even
 
     def forwards(t):
         if t in late:
@@ -211,6 +212,13 @@
             put(ge, g_in[...], every, every)
 
         put(a, product(get(ge, every, every), get(go, every, every)), every, every)
+
+        @pl.when(ahead)
+        def _():
+            for t in range(sends // 2):
+                send_down(t).wait_recv()
+                send_side(t).start()
+
         pl.when(is_even)(receive_c_odd)
         k_value = product(split(c_odd[...]), get(ge, mine, every), True)
         k_half[...] = k_value
@@ -240,8 +248,12 @@
 
         used = 0
         for t in range(sends):
-            send_down(t).wait_recv()
-            pl.when(forwards(t))(send_side(t).start)
+            if t in late:
+                send_down(t).wait_recv()
+                pl.when(forwards(t))(send_side(t).start)
+            else:
+                pl.when(jnp.logical_not(ahead))(send_down(t).wait_recv)
+                pl.when(jnp.logical_not(second))(send_side(t).start)
             if t % PIECES == 0 and t >= 2 * PIECES:
                 use(used)
                 used += 1

time: 115 us -> 110 us (0.957)
  Pallas kernels: 110 us -> 105 us
    pallas_call x1, Pallas kernels: 110 us -> 105 us  [on_device(): pl.pallas_call(functools.partial(kernel, n), out_shape=(jax.ShapeDtypeStr...]
where the time goes in v5:
time: 110 us; the launch traced here: 109 us
  Pallas kernels  105 us (95%)
  local copies, waits for them, and re-layouts  3.32 us (3%)
    pallas_call x1, Pallas kernels, on_device(): pl.pallas_call(functools.partial(kernel, n), out_shape=(jax.ShapeDtypeStr...  105 us
    unnamed x4, local copies, waits for them, and re-layouts  3.32 us

profile of v5, /device:TPU:26, one launch (start us, length us, event | category | flops | bytes accessed | tf_op | source)
XLA Modules:
  0.0 109.4 jit_solution(10781901454636368615)
XLA Ops:
  0.6 105.4 %shard_map.50 = (f32[1,512,512]{2,1,0:T(8,128)}, f32[512,512]{1,0:T(8,128)}) custom-call(f32[1,512,512]{2,1,0:T(8,128)} %g_ref.1, f32[1,512,512]{2,1,0:T(8,128)} %c_ref.1, f32[512,512]{1,0:T(8,128)} %f_ref.1), custom_call_target="tpu_custom_call" | custom-call | tf_op jit(solution)/shard_map/pallas_call | solution.py:384
  106.0 0.0 copy-start
  106.0 2.4 %copy.7 = f32[1,512,512]{2,1,0:T(8,128)} copy(f32[1,512,512]{2,1,0:T(8,128)} %get-tuple-element.4) | data formatting | bytes 2097152
  108.4 0.0 copy-done
  108.4 1.0 copy.8
Async XLA Ops:
  106.0 2.4 %copy-start = (f32[512,512]{1,0:T(8,128)S(1)}, f32[512,512]{1,0:T(8,128)}, u32[]{:S(2)}) copy-start(f32[512,512]{1,0:T(8,128)} %get-tuple-element.5) | copy-start | bytes 3145732
